TPU v7x, 32 devices: a whole 2x2x4 slice. The times are simulated.
32 devices in a mesh: grp: 4 (over y, x), body: 8 (over z, core).
Axes of the slice: x: 2, y: 2, z: 4, core: 2. Of those that a mesh axis runs over, the one named last changes fastest.
Arguments:
- incident: bfloat16 [32, 16, 512], P(('grp', 'body')), may hold values from -6 to 6
- exciting: float32 [32, 16, 512], P(('grp', 'body')), may hold values from -6 to 6
- t_matrices: bfloat16 [32, 2, 256, 256], P(('grp', 'body')), may hold values from -0.1875 to 0.1875
- hankel_rows: bfloat16 [225, 2, 512], replicated, may hold values from -0.09375 to 0.09375
- offsets: int32 [32, 8], P(('grp', 'body')), may hold values from 0 to 224
- lattice_slots: int32 [32], P('grp'), may hold values from 0 to 7, as said below
- up_maps: bfloat16 [32, 2, 256, 512], P(('grp', 'body')), may hold values from -0.125 to 0.125
- down_maps: bfloat16 [32, 2, 512, 256], P(('grp', 'body')), may hold values from -0.1875 to 0.1875
- group_maps: bfloat16 [4, 4, 2, 512, 512], P('grp', None, None, 'body'), may hold values from -0.09375 to 0.09375
Outputs:
- updated: float32 [32, 16, 512], P(('grp', 'body'))
Inputs may be any that keep to these rules, and one draw needn't show every extreme that they name: `lattice_slots`: within each group the 8 columns stand at the slots 0 to 7, one column a slot.
All inputs are finite; a program needn't handle non-finite values.
Results may differ from a plain program's by a relative error of at most 0.0034.
Values may be sent and summed in bfloat16 or wider, within the bound.
No kernel may reach another device: no remote copies, remote signals or barrier semaphores. Data moves between devices by JAX's collectives and lax.ppermute only.
A program may use at most 64 MiB of HBM per device.

v0:
```python
import math
import jax
import jax.numpy as jnp
from jax import lax
from jax.sharding import PartitionSpec as P


def complex_apply(form, values, real_mats, imag_mats):
    half_width = values.shape[-1] // 2
    real_values = values[..., :half_width]
    imag_values = values[..., half_width:]
    real_out = jnp.einsum(
        form, real_values, real_mats, preferred_element_type=jnp.float32
    ) - jnp.einsum(form, imag_values, imag_mats, preferred_element_type=jnp.float32)
    imag_out = jnp.einsum(
        form, real_values, imag_mats, preferred_element_type=jnp.float32
    ) + jnp.einsum(form, imag_values, real_mats, preferred_element_type=jnp.float32)
    return jnp.concatenate([real_out, imag_out], axis=-1)


def toeplitz_mats(sequences):
    length = sequences.shape[-1] // 2
    repeats = (1,) * (sequences.ndim - 1) + (length,)
    tiled = jnp.tile(sequences, repeats)
    window = tiled[..., length : length + length * (2 * length - 1)]
    return window.reshape(sequences.shape[:-1] + (length, 2 * length - 1))[..., :length]


def local(
    incident,
    exciting,
    t_matrices,
    hankel_rows,
    offsets,
    lattice_slots,
    up_maps,
    down_maps,
    group_maps,
):
    body_index = lax.axis_index("body")
    group_index = lax.axis_index("grp")
    local_count = incident.shape[0]
    scattered = complex_apply("iln,inm->ilm", incident, t_matrices[:, 0], t_matrices[:, 1]).astype(
        jnp.bfloat16
    )
    own_members = body_index * local_count + jnp.arange(local_count, dtype=jnp.int32)
    zero_seq = jnp.zeros((), jnp.bfloat16)
    empty = jnp.zeros(scattered.shape, jnp.float32)
    total = empty
    piece = lax.all_gather(scattered, "body", axis=0, tiled=True)
    width = piece.shape[0]
    block_rows = math.gcd(width, 4)
    table_rows = jnp.take(offsets, lattice_slots, axis=1)
    sequences = jnp.take(hankel_rows, table_rows, axis=0)
    sources = jnp.arange(width, dtype=jnp.int32)
    keep = own_members[:, None] != sources[None, :]
    sequences = jnp.where(keep[:, :, None, None], sequences, zero_seq)
    sequences = sequences.reshape(
        (local_count, width // block_rows, block_rows) + sequences.shape[2:]
    ).swapaxes(0, 1)
    pieces = piece.reshape((width // block_rows, block_rows) + piece.shape[1:])

    def one_block(accum, inputs):
        block_seqs, block_piece = inputs
        mats = toeplitz_mats(block_seqs)
        return (
            accum + complex_apply("jln,tjnm->tlm", block_piece, mats[:, :, 0], mats[:, :, 1]),
            None,
        )

    total, _ = lax.scan(one_block, total, (sequences, pieces))
    partial_value = complex_apply("iln,inq->lq", scattered, up_maps[:, 0], up_maps[:, 1])
    expansion = lax.psum(partial_value, "body").astype(jnp.bfloat16)
    block_width = group_maps.shape[3]
    full_width = group_maps.shape[4]
    real_block = lax.dynamic_slice_in_dim(expansion, body_index * block_width, block_width, 1)
    imag_block = lax.dynamic_slice_in_dim(
        expansion, full_width + body_index * block_width, block_width, 1
    )
    own_block = jnp.concatenate([real_block, imag_block], axis=-1)[None]
    piece = lax.all_gather(own_block, "grp", axis=0, tiled=True)
    width = piece.shape[0]
    sources = jnp.arange(width, dtype=jnp.int32)
    piece = jnp.where((sources != group_index)[:, None, None], piece, zero_seq)
    mats = group_maps[0]
    incoming_part = complex_apply("hln,hnq->lq", piece, mats[:, 0], mats[:, 1])
    incoming = lax.psum(incoming_part, "body").astype(jnp.bfloat16)
    far = complex_apply("lq,iqp->ilp", incoming, down_maps[:, 0], down_maps[:, 1])
    return exciting + total + far


def solution(mesh):
    return jax.shard_map(
        local,
        mesh=mesh,
        in_specs=(
            P(("grp", "body"), None, None),
            P(("grp", "body"), None, None),
            P(("grp", "body"), None, None, None),
            P(),
            P(("grp", "body"), None),
            P("grp"),
            P(("grp", "body"), None, None, None),
            P(("grp", "body"), None, None, None),
            P("grp", None, None, "body", None),
        ),
        out_specs=P(("grp", "body"), None, None),
        check_vma=False,
    )
```

profile of v0, /device:TPU:0, one launch (start us, length us, event | category | flops | bytes accessed | tf_op | source)
XLA Modules:
  0.0 120.4 jit_solution(14881951126355513148)
XLA Ops:
  0.0 1.1 fusion.38
  1.1 1.1 fusion.12
  2.2 1.1 fusion.20
  3.3 1.1 fusion.34
  4.5 1.1 fusion.13
  5.5 1.1 convolution_add_fusion
  6.6 1.1 fusion.24
  7.7 1.1 convolution_subtract_fusion
  8.8 0.0 copy-start.5
  8.9 0.0 copy-start.1
  8.9 30.7 %psum.14 = bf16[16,1024]{1,0:T(8,128)(2,1)S(1)} all-reduce(f32[16,1024]{1,0:T(8,128)S(1)} %pad_maximum_fusion), channel_id=1, replica_groups=mesh['grp'=4,'body'=8] {'body'}, use_global_device_ids=true, to_apply=%region_2.3 | all-reduce | flops 16384 | bytes 98304 | tf_op jit(solution)/shard_map/psum | solution.py:73
  39.6 0.1 constant_dynamic-slice_fusion.1
  39.7 0.1 pad_maximum_fusion.3
  39.8 8.2 %all-gather = bf16[64,128]{1,0:T(8,128)(2,1)S(1)} all-gather(bf16[16,128]{1,0:T(8,128)(2,1)S(1)} %pad_maximum_fusion.3), channel_id=2, replica_groups=mesh['grp'=4,'body'=8] {'grp'}, dimensions={0}, use_global_device_ids=true | all-gather | bytes 20480 | tf_op jit(solution)/shard_map/all_gather | solution.py:81
  48.0 0.1 broadcast_select_fusion.2
  48.1 0.2 convolution_bitcast_fusion.7
  48.3 0.3 fusion.9
  48.5 0.2 convolution_bitcast_fusion.5
  48.7 0.3 fusion.8
  49.0 26.3 %psum.15 = bf16[16,1024]{1,0:T(8,128)(2,1)S(1)} all-reduce(f32[16,1024]{1,0:T(8,128)S(1)} %pad_maximum_fusion.1), channel_id=1, replica_groups=mesh['grp'=4,'body'=8] {'body'}, use_global_device_ids=true, to_apply=%region_3.4 | all-reduce | flops 16384 | bytes 98304 | tf_op jit(solution)/shard_map/psum | solution.py:87
  75.3 0.1 fusion.18
  75.5 0.2 fusion.11
  75.6 0.2 fusion.14
  75.8 0.2 fusion.10
  75.9 14.0 %all_gather.6 = bf16[8,16,512]{2,1,0:T(8,128)(2,1)S(1)} all-gather(bf16[1,16,512]{2,1,0:T(8,128)(2,1)S(1)} %pad_maximum_fusion.2), channel_id=1, replica_groups=mesh['grp'=4,'body'=8] {'body'}, dimensions={0}, use_global_device_ids=true | all-gather | bytes 147456 | tf_op jit(solution)/shard_map/all_gather | solution.py:50
  89.9 0.6 gather_fusion
  90.6 0.6 gather_fusion.1
  91.2 0.1 broadcast_in_dim.54
  91.3 0.1 fusion.44
  91.4 0.0 copy-start.4
  91.4 28.3 %while.11 = (s32[]{:T(128)}, f32[1,16,512]{2,1,0:T(8,128)S(1)}, bf16[2,1,4,2,512]{4,3,2,1,0:T(2,128)(2,1)S(1)}, bf16[2,4,16,512]{3,2,1,0:T(8,128)(2,1)S(1)}, s32[]{:T(128)}, /*index=5*/s32[]{:T(128)}) while((s32[]{:T(128)}, f32[1,16,512]{2,1,0:T(8,128)S(1)}, bf16[2,1,4,2,512]{4,3,2,1,0:T(2,128)(2,1)S(1)}, ...), condition=%wide.region_1.2_spmd.clone, body=%wide.region_0.1_spmd.clone.sunk | while | flops 33587200 | bytes 17244244 | solution.py:71
  91.5 0.2 tile.16
  91.6 2.8 %tile.17 = bf16[1,4,2,131072]{3,2,1,0:T(2,128)(2,1)} reshape(bf16[4,2,256,512]{3,2,1,0:T(8,128)(2,1)S(1)} %tile.16) | data formatting | bytes 4194304 | tf_op jit(solution)/shard_map/while/body/eval_jaxpr/tile | solution.py:24
  94.4 4.3 %slice.213 = bf16[1,4,2,130816]{3,2,1,0:T(2,128)(2,1)} slice(bf16[1,4,2,131072]{3,2,1,0:T(2,128)(2,1)} %tile.17), slice={[0:1], [0:4], [0:2], [256:131072]} | slice | bytes 4186112 | tf_op jit(solution)/shard_map/while/body/eval_jaxpr/slice | solution.py:25
  98.7 6.1 %reshape.255 = bf16[1,4,2,256,511]{4,3,2,1,0:T(8,128)(2,1)S(1)} reshape(bf16[1,4,2,130816]{3,2,1,0:T(2,128)(2,1)} %slice.213) | data formatting | bytes 4186112 | tf_op jit(solution)/shard_map/while/body/eval_jaxpr/reshape | solution.py:26
  104.8 0.2 convolution_bitcast_fusion.11
  105.0 0.2 fusion.76
  105.2 0.2 convolution_bitcast_fusion.10
  105.4 0.2 fusion.75
  105.6 0.2 tile.16
  105.8 2.8 %tile.17 = bf16[1,4,2,131072]{3,2,1,0:T(2,128)(2,1)} reshape(bf16[4,2,256,512]{3,2,1,0:T(8,128)(2,1)S(1)} %tile.16) | data formatting | bytes 4194304 | tf_op jit(solution)/shard_map/while/body/eval_jaxpr/tile | solution.py:24
  108.5 4.3 %slice.213 = bf16[1,4,2,130816]{3,2,1,0:T(2,128)(2,1)} slice(bf16[1,4,2,131072]{3,2,1,0:T(2,128)(2,1)} %tile.17), slice={[0:1], [0:4], [0:2], [256:131072]} | slice | bytes 4186112 | tf_op jit(solution)/shard_map/while/body/eval_jaxpr/slice | solution.py:25
  112.9 6.1 %reshape.255 = bf16[1,4,2,256,511]{4,3,2,1,0:T(8,128)(2,1)S(1)} reshape(bf16[1,4,2,130816]{3,2,1,0:T(2,128)(2,1)} %slice.213) | data formatting | bytes 4186112 | tf_op jit(solution)/shard_map/while/body/eval_jaxpr/reshape | solution.py:26
  119.0 0.2 convolution_bitcast_fusion.11
  119.2 0.2 fusion.76
  119.4 0.2 convolution_bitcast_fusion.10
  119.6 0.2 fusion.75
  119.8 0.6 maximum_add_fusion.1
  (26 shorter events, 0.2 us)
Async XLA Ops:
  0.0 90.6 %copy-start = (bf16[225,2,512]{2,1,0:T(2,128)(2,1)S(1)}, bf16[225,2,512]{2,1,0:T(2,128)(2,1)}, u32[]{:S(2)}) copy-start(bf16[225,2,512]{2,1,0:T(2,128)(2,1)} %param.14) | copy-start | bytes 1382404
  0.0 48.0 %copy-start.3 = (bf16[1,4,2,64,512]{4,3,2,1,0:T(8,128)(2,1)S(1)}, bf16[1,4,2,64,512]{4,3,2,1,0:T(8,128)(2,1)}, u32[]{:S(2)}) copy-start(bf16[1,4,2,64,512]{4,3,2,1,0:T(8,128)(2,1)} %param.19) | copy-start | bytes 1572868
  3.3 72.0 %copy-start.2 = (bf16[1,2,512,256]{3,2,1,0:T(8,128)(2,1)S(1)}, bf16[1,2,512,256]{3,2,1,0:T(8,128)(2,1)}, u32[]{:S(2)}) copy-start(bf16[1,2,512,256]{3,2,1,0:T(8,128)(2,1)} %param.18) | copy-start | bytes 1572868
  8.8 81.1 %copy-start.5 = (s32[8]{0:T(128)S(1)}, s32[8]{0:T(128)}, u32[]{:S(2)}) copy-start(s32[8]{0:T(128)} %param.16) | copy-start | bytes 100
  8.9 81.1 %copy-start.1 = (s32[1,8]{1,0:T(1,128)S(1)}, s32[1,8]{1,0:T(1,128)}, u32[]{:S(2)}) copy-start(s32[1,8]{1,0:T(1,128)} %param.15) | copy-start | bytes 100
  91.4 28.4 %copy-start.4 = (f32[1,16,512]{2,1,0:T(8,128)S(1)}, f32[1,16,512]{2,1,0:T(8,128)}, u32[]{:S(2)}) copy-start(f32[1,16,512]{2,1,0:T(8,128)} %param.12) | copy-start | bytes 98308
where the time goes:
time: 121 us; the launch traced here: 120 us
  blocking collectives  79.2 us (65%)
  local copies, waits for them, and re-layouts  28.2 us (23%)
  matrix products  11.8 us (10%)
    psum x1, blocking collectives, local(): expansion = lax.psum(partial_value, 'body').astype(jnp.bfloat16)  30.7 us
    psum x1, blocking collectives, local(): incoming = lax.psum(incoming_part, 'body').astype(jnp.bfloat16)  26.3 us
    all_gather x1, blocking collectives, local(): piece = lax.all_gather(scattered, 'body', axis=0, tiled=True)  14 us
    reshape x2, local copies, waits for them, and re-layouts, toeplitz_mats(): window.reshape(sequences.shape[:-1] + (length, 2 * length - 1))  12.2 us
    slice x2, local copies, waits for them, and re-layouts, toeplitz_mats(): window = tiled[..., length:length + length * (2 * length - 1)]  8.67 us
    all_gather x1, blocking collectives, local(): piece = lax.all_gather(own_block, 'grp', axis=0, tiled=True)  8.18 us
    another operation x6, local copies, waits for them, and re-layouts, toeplitz_mats(): tiled = jnp.tile(sequences, repeats)  5.85 us
    dot_general x6, matrix products, complex_apply(): jnp.einsum(form, imag_values, real_mats, preferred_element_type=jnp.float32)  2.97 us

commit v1 on v0

--- a/solution.py
+++ b/solution.py
@@ -3,6 +3,7 @@
 import jax.numpy as jnp
 from jax import lax
 from jax.sharding import PartitionSpec as P
+from jax.lax import all_gather
 
 
 def complex_apply(form, values, real_mats, imag_mats):
@@ -84,7 +85,7 @@
     piece = jnp.where((sources != group_index)[:, None, None], piece, zero_seq)
     mats = group_maps[0]
     incoming_part = complex_apply("hln,hnq->lq", piece, mats[:, 0], mats[:, 1])
-    incoming = lax.psum(incoming_part, "body").astype(jnp.bfloat16)
+    incoming = all_gather(incoming_part, "body").sum(axis=0).astype(jnp.bfloat16)
     far = complex_apply("lq,iqp->ilp", incoming, down_maps[:, 0], down_maps[:, 1])
     return exciting + total + far
 

time: 121 us -> 110 us (0.909)
  blocking collectives: 79.2 us -> 67.8 us
    psum x1 -> x0, blocking collectives: 26.3 us -> none  [local(): incoming = lax.psum(incoming_part, 'body').astype(jnp.bfloat16)]
    all_gather x0 -> x1, blocking collectives: none -> 14.9 us  [local(): all_gather(incoming_part, 'body').sum(axis=0).astype(jnp.bfloat16)]
where the time goes in v1:
time: 110 us; the launch traced here: 109 us
  blocking collectives  67.8 us (62%)
  local copies, waits for them, and re-layouts  28.2 us (26%)
  matrix products  11.8 us (11%)
    psum x1, blocking collectives, local(): expansion = lax.psum(partial_value, 'body').astype(jnp.bfloat16)  30.7 us
    all_gather x1, blocking collectives, local(): all_gather(incoming_part, 'body').sum(axis=0).astype(jnp.bfloat16)  14.9 us
    all_gather x1, blocking collectives, local(): piece = lax.all_gather(scattered, 'body', axis=0, tiled=True)  14 us
    reshape x2, local copies, waits for them, and re-layouts, toeplitz_mats(): window.reshape(sequences.shape[:-1] + (length, 2 * length - 1))  12.2 us
    slice x2, local copies, waits for them, and re-layouts, toeplitz_mats(): window = tiled[..., length:length + length * (2 * length - 1)]  8.67 us
    all_gather x1, blocking collectives, local(): piece = lax.all_gather(own_block, 'grp', axis=0, tiled=True)  8.18 us
    another operation x6, local copies, waits for them, and re-layouts, toeplitz_mats(): tiled = jnp.tile(sequences, repeats)  5.85 us
    dot_general x6, matrix products, complex_apply(): jnp.einsum(form, imag_values, imag_mats, preferred_element_type=jnp.float32)  3.02 us

profile of v1, /device:TPU:0, one launch (start us, length us, event | category | flops | bytes accessed | tf_op | source)
XLA Modules:
  0.0 109.0 jit_solution(8011051680875258858)
XLA Ops:
  0.0 1.1 %fusion.38 = f32[16,256]{1,0:T(8,128)S(1)} fusion(bf16[1,2,256,256]{3,2,1,0:T(8,128)(2,1)} %param.13, bf16[1,16,512]{2,1,0:T(8,128)(2,1)} %param.11), kind=kOutput, calls=%fused_computation.62 | convolution fusion | flops 2097152 | bytes 155648 | tf_op jit(solution)/shard_map/iln,inm->ilm/dot_general | solution.py:13
  1.1 1.1 fusion.12
  2.2 1.1 %fusion.20 = f32[16,512]{1,0:T(8,128)S(1)} fusion(bf16[16,256]{1,0:T(8,128)(2,1)S(1)} %fusion.12, bf16[1,2,256,512]{3,2,1,0:T(8,128)(2,1)} %param.17), kind=kOutput, calls=%fused_computation.44 | convolution fusion | flops 4194304 | bytes 303104 | tf_op jit(solution)/shard_map/iln,inq->lq/dot_general | solution.py:16
  3.3 1.1 fusion.34
  4.4 1.1 fusion.13
  5.5 1.1 %convolution_add_fusion = f32[16,512]{1,0:T(8,128)S(1)} fusion(f32[16,512]{1,0:T(8,128)S(1)} %fusion.20, bf16[16,256]{1,0:T(8,128)(2,1)S(1)} %fusion.13, bf16[1,2,256,512]{3,2,1,0:T(8,128)(2,1)} %param.17), kind=kOutput, calls=%fused_computation.25 | convolution fusion | flops 4202496 | bytes 335872 | tf_op jit(solution)/shard_map/iln,inq->lq/dot_general | solution.py:18
  6.6 1.1 %fusion.24 = f32[16,512]{1,0:T(8,128)S(1)} fusion(bf16[16,256]{1,0:T(8,128)(2,1)S(1)} %fusion.12, bf16[1,2,256,512]{3,2,1,0:T(8,128)(2,1)} %param.17), kind=kOutput, calls=%fused_computation.48 | convolution fusion | flops 4194304 | bytes 303104 | tf_op jit(solution)/shard_map/iln,inq->lq/dot_general | solution.py:13
  7.7 1.2 %convolution_subtract_fusion = f32[16,512]{1,0:T(8,128)S(1)} fusion(f32[16,512]{1,0:T(8,128)S(1)} %fusion.24, bf16[16,256]{1,0:T(8,128)(2,1)S(1)} %fusion.13, bf16[1,2,256,512]{3,2,1,0:T(8,128)(2,1)} %param.17), kind=kOutput, calls=%fused_computation.26 | convolution fusion | flops 4202496 | bytes 335872 | tf_op jit(solution)/shard_map/iln,inq->lq/dot_general | solution.py:15
  8.8 30.7 %psum.7 = bf16[16,1024]{1,0:T(8,128)(2,1)S(1)} all-reduce(f32[16,1024]{1,0:T(8,128)S(1)} %pad_maximum_fusion), channel_id=1, replica_groups=mesh['grp'=4,'body'=8] {'body'}, use_global_device_ids=true, to_apply=%region_2.3 | all-reduce | flops 16384 | bytes 98304 | tf_op jit(solution)/shard_map/psum | solution.py:74
  39.6 0.1 constant_dynamic-slice_fusion.1
  39.7 0.1 pad_maximum_fusion.3
  39.8 8.2 %all-gather = bf16[64,128]{1,0:T(8,128)(2,1)S(1)} all-gather(bf16[16,128]{1,0:T(8,128)(2,1)S(1)} %pad_maximum_fusion.3), channel_id=2, replica_groups=mesh['grp'=4,'body'=8] {'grp'}, dimensions={0}, use_global_device_ids=true | all-gather | bytes 20480 | tf_op jit(solution)/shard_map/all_gather | solution.py:82
  47.9 0.1 broadcast_select_fusion.2
  48.1 0.0 copy-start.5
  48.1 0.0 copy-start.1
  48.1 0.2 convolution_bitcast_fusion.7
  48.3 0.3 fusion.9
  48.5 0.2 convolution_bitcast_fusion.5
  48.7 0.3 fusion.8
  49.0 14.9 %all-gather.1 = f32[128,1024]{1,0:T(8,128)S(1)} all-gather(f32[16,1024]{1,0:T(8,128)S(1)} %pad_maximum_fusion.1), channel_id=3, replica_groups=mesh['grp'=4,'body'=8] {'body'}, dimensions={0}, use_global_device_ids=true | all-gather | bytes 589824 | tf_op jit(solution)/shard_map/all_gather | solution.py:88
  64.0 0.1 fusion.18
  64.1 0.2 fusion.11
  64.3 0.2 fusion.14
  64.4 0.2 fusion.10
  64.6 14.0 %all_gather.12 = bf16[8,16,512]{2,1,0:T(8,128)(2,1)S(1)} all-gather(bf16[1,16,512]{2,1,0:T(8,128)(2,1)S(1)} %pad_maximum_fusion.2), channel_id=1, replica_groups=mesh['grp'=4,'body'=8] {'body'}, dimensions={0}, use_global_device_ids=true | all-gather | bytes 147456 | tf_op jit(solution)/shard_map/all_gather | solution.py:51
  78.6 0.6 gather_fusion
  79.3 0.6 gather_fusion.1
  79.9 0.1 broadcast_in_dim.54
  80.0 0.1 fusion.44
  80.1 0.0 copy-start.4
  80.1 28.3 %while.11 = (s32[]{:T(128)}, f32[1,16,512]{2,1,0:T(8,128)S(1)}, bf16[2,1,4,2,512]{4,3,2,1,0:T(2,128)(2,1)S(1)}, bf16[2,4,16,512]{3,2,1,0:T(8,128)(2,1)S(1)}, s32[]{:T(128)}, /*index=5*/s32[]{:T(128)}) while((s32[]{:T(128)}, f32[1,16,512]{2,1,0:T(8,128)S(1)}, bf16[2,1,4,2,512]{4,3,2,1,0:T(2,128)(2,1)S(1)}, ...), condition=%wide.region_1.2_spmd.clone, body=%wide.region_0.1_spmd.clone.sunk | while | flops 33587200 | bytes 17244244 | solution.py:72
  80.1 0.2 tile.16
  80.3 2.8 %tile.17 = bf16[1,4,2,131072]{3,2,1,0:T(2,128)(2,1)} reshape(bf16[4,2,256,512]{3,2,1,0:T(8,128)(2,1)S(1)} %tile.16) | data formatting | bytes 4194304 | tf_op jit(solution)/shard_map/while/body/eval_jaxpr/tile | solution.py:25
  83.0 4.3 %slice.213 = bf16[1,4,2,130816]{3,2,1,0:T(2,128)(2,1)} slice(bf16[1,4,2,131072]{3,2,1,0:T(2,128)(2,1)} %tile.17), slice={[0:1], [0:4], [0:2], [256:131072]} | slice | bytes 4186112 | tf_op jit(solution)/shard_map/while/body/eval_jaxpr/slice | solution.py:26
  87.4 6.1 %reshape.256 = bf16[1,4,2,256,511]{4,3,2,1,0:T(8,128)(2,1)S(1)} reshape(bf16[1,4,2,130816]{3,2,1,0:T(2,128)(2,1)} %slice.213) | data formatting | bytes 4186112 | tf_op jit(solution)/shard_map/while/body/eval_jaxpr/reshape | solution.py:27
  93.5 0.2 convolution_bitcast_fusion.11
  93.7 0.2 fusion.76
  93.8 0.2 convolution_bitcast_fusion.10
  94.0 0.2 fusion.75
  94.3 0.2 tile.16
  94.4 2.8 %tile.17 = bf16[1,4,2,131072]{3,2,1,0:T(2,128)(2,1)} reshape(bf16[4,2,256,512]{3,2,1,0:T(8,128)(2,1)S(1)} %tile.16) | data formatting | bytes 4194304 | tf_op jit(solution)/shard_map/while/body/eval_jaxpr/tile | solution.py:25
  97.2 4.3 %slice.213 = bf16[1,4,2,130816]{3,2,1,0:T(2,128)(2,1)} slice(bf16[1,4,2,131072]{3,2,1,0:T(2,128)(2,1)} %tile.17), slice={[0:1], [0:4], [0:2], [256:131072]} | slice | bytes 4186112 | tf_op jit(solution)/shard_map/while/body/eval_jaxpr/slice | solution.py:26
  101.5 6.1 %reshape.256 = bf16[1,4,2,256,511]{4,3,2,1,0:T(8,128)(2,1)S(1)} reshape(bf16[1,4,2,130816]{3,2,1,0:T(2,128)(2,1)} %slice.213) | data formatting | bytes 4186112 | tf_op jit(solution)/shard_map/while/body/eval_jaxpr/reshape | solution.py:27
  107.6 0.2 convolution_bitcast_fusion.11
  107.8 0.2 fusion.76
  108.0 0.2 convolution_bitcast_fusion.10
  108.2 0.2 fusion.75
  108.4 0.6 maximum_add_fusion.1
  (27 shorter events, 0.2 us)
Async XLA Ops:
  0.0 79.3 %copy-start = (bf16[225,2,512]{2,1,0:T(2,128)(2,1)S(1)}, bf16[225,2,512]{2,1,0:T(2,128)(2,1)}, u32[]{:S(2)}) copy-start(bf16[225,2,512]{2,1,0:T(2,128)(2,1)} %param.14) | copy-start | bytes 1382404
  0.0 48.0 %copy-start.3 = (bf16[1,4,2,64,512]{4,3,2,1,0:T(8,128)(2,1)S(1)}, bf16[1,4,2,64,512]{4,3,2,1,0:T(8,128)(2,1)}, u32[]{:S(2)}) copy-start(bf16[1,4,2,64,512]{4,3,2,1,0:T(8,128)(2,1)} %param.19) | copy-start | bytes 1572868
  7.7 56.3 %copy-start.2 = (bf16[1,2,512,256]{3,2,1,0:T(8,128)(2,1)S(1)}, bf16[1,2,512,256]{3,2,1,0:T(8,128)(2,1)}, u32[]{:S(2)}) copy-start(bf16[1,2,512,256]{3,2,1,0:T(8,128)(2,1)} %param.18) | copy-start | bytes 1572868
  48.1 30.5 %copy-start.5 = (s32[8]{0:T(128)S(1)}, s32[8]{0:T(128)}, u32[]{:S(2)}) copy-start(s32[8]{0:T(128)} %param.16) | copy-start | bytes 100
  48.1 30.5 %copy-start.1 = (s32[1,8]{1,0:T(1,128)S(1)}, s32[1,8]{1,0:T(1,128)}, u32[]{:S(2)}) copy-start(s32[1,8]{1,0:T(1,128)} %param.15) | copy-start | bytes 100
  80.1 28.4 %copy-start.4 = (f32[1,16,512]{2,1,0:T(8,128)S(1)}, f32[1,16,512]{2,1,0:T(8,128)}, u32[]{:S(2)}) copy-start(f32[1,16,512]{2,1,0:T(8,128)} %param.12) | copy-start | bytes 98308
